TPU v7x, 512 devices: a whole 4x4x16 slice. The times are simulated.
512 devices in a mesh: cells: 128 (over z, y, core), mem: 4 (over x).
Axes of the slice: x: 4, y: 4, z: 16, core: 2. Of those that a mesh axis runs over, the one named last changes fastest.
Arguments:
- ensemble: float32 [512, 262144], P('mem', 'cells'), may hold values from -6 to 6
- observed: float32 [262144], P('cells'), may hold values from -6 to 6
- obs_sigma: float32 [262144], P('cells'), may hold values from 0.1 to 1
- obs_index: int32 [262144], P('cells'), may hold values from 0 to 2047
- member_seeds: int32 [512], P('mem'), may hold values from 1 to 65520
Outputs:
- updated: float32 [512, 262144], P('mem', 'cells')
All inputs are finite; a program needn't handle non-finite values.
Results may differ from a plain program's by a relative error of at most 0.0003.
Values sent between devices are 32-bit elements; how exact they have to be, the bound alone decides.
A program may use at most 64 MiB of HBM per device.

v0:
```python
import math
import jax
import jax.numpy as jnp
from jax import lax
from jax.sharding import Mesh
from jax.sharding import PartitionSpec as P

SECTION = 1
CELLS = ("cells_0", "cells_1", "cells_2")
plan = (28.0 / 3.0, 7.0, 4.0, 2.0)


def from_everyone(shard, axis):
    copies = jnp.broadcast_to(shard, (lax.axis_size(axis), *shard.shape))
    return lax.all_to_all(copies, axis, split_axis=0, concat_axis=0, tiled=True)


def over_copies(shard, axis):
    return from_everyone(shard, axis).sum(axis=0)


def together(arrays, axis):
    ends = [0]
    for a in arrays:
        ends.append(ends[-1] + a.size)
    total = over_copies(jnp.concatenate([a.ravel() for a in arrays]), axis)
    return tuple((total[b:e].reshape(a.shape) for a, b, e in zip(arrays, ends, ends[1:])))


def rows_for(lines, devices):
    spare = -len(lines) % devices
    return jnp.pad(lines, [(0, spare)] + [(0, 0)] * (lines.ndim - 1))


def laid_out(tiles, dim):
    tiles = jnp.moveaxis(tiles, 0, dim)
    lengths = tiles.shape
    return tiles.reshape(*lengths[:dim], lengths[dim] * lengths[dim + 1], *lengths[dim + 2 :])


def gather_axes(shard, axes, dim):
    far, near = axes
    leading = from_everyone(shard, far)
    tiles = jnp.swapaxes(from_everyone(leading, near), 0, 1)
    return laid_out(tiles.reshape(-1, *shard.shape), dim)


def in_blocks(shard, dim, devices):
    lengths = shard.shape
    tiles = shard.reshape(*lengths[:dim], devices, lengths[dim] // devices, *lengths[dim + 1 :])
    return jnp.moveaxis(tiles, dim, 0)


def summed_on_arrival(shard, axis, dim):
    devices = lax.axis_size(axis)
    tiles = lax.all_to_all(in_blocks(shard, dim, devices), axis, 0, 0, tiled=True)
    return jnp.sum(tiles, axis=0)


def summed_rows(shard, axes, dim):
    far, near = axes
    tiles = in_blocks(shard, dim, lax.axis_size(far))
    nearer = summed_on_arrival(tiles, near, dim + 1)
    arrived = lax.all_to_all(nearer, far, split_axis=0, concat_axis=0, tiled=True)
    return arrived.sum(axis=0)


def nested_sum(shard, axes):
    padded = rows_for(shard, lax.axis_size(axes[0]) * lax.axis_size(axes[1]))
    whole = gather_axes(summed_rows(padded, axes, 0), axes, 0)
    return lax.slice_in_dim(whole, 0, len(shard)).reshape(shard.shape)


def together_2(arrays, axis):
    ends = [0]
    for a in arrays:
        ends.append(ends[-1] + a.size)
    total = nested_sum(jnp.concatenate([a.ravel() for a in arrays]), axis)
    return tuple((total[b:e].reshape(a.shape) for a, b, e in zip(arrays, ends, ends[1:])))


def perturbation(member_seeds, positions):
    seeds_col = member_seeds[:, None]
    where_row = positions[None, :]
    hashed = (seeds_col * 389 % 65521 + where_row % 65521 * (seeds_col % 997 + 1)) % 65521
    return math.sqrt(2.0) * jnp.cos(2.0 * math.pi / 65521.0 * hashed.astype(jnp.float32))


def shards(ensemble, observed, obs_sigma, obs_index, member_seeds):
    highest = lax.Precision.HIGHEST
    own_members, cell_count = ensemble.shape
    obs_count = observed.shape[0]
    members = own_members * lax.axis_size("mem")
    alpha = jnp.float32(plan[SECTION])
    value = ensemble[:, obs_index]
    predicted = jnp.tanh(value) + 0.5 * value
    totals = together((jnp.sum(ensemble, axis=0), jnp.sum(predicted, axis=0)), "mem")
    mean_state = totals[0] / members
    mean_pred = totals[1] / members
    positions = lax.axis_index(CELLS) * obs_count + jnp.arange(obs_count, dtype=jnp.int32)
    noise = perturbation(member_seeds, positions)
    scaled = (predicted - mean_pred) / (obs_sigma * math.sqrt(members - 1.0))
    innovation = observed / obs_sigma + jnp.sqrt(alpha) * noise - predicted / obs_sigma
    gathered = lax.all_gather(scaled, "mem", axis=0, tiled=True)
    gram_matrix, cross_terms = together_2(
        (
            jnp.dot(gathered, gathered.T, precision=highest),
            jnp.dot(gathered, innovation.T, precision=highest),
        ),
        (("cells_0", "cells_1"), "cells_2"),
    )
    factor = jnp.linalg.cholesky(gram_matrix + alpha * jnp.eye(members, dtype=jnp.float32))
    weights = jax.scipy.linalg.cho_solve((factor, True), cross_terms)
    anomalies = ensemble - mean_state
    change = jnp.zeros((own_members, cell_count), jnp.float32) + jnp.dot(
        weights.T, lax.all_gather(anomalies, "mem", axis=0, tiled=True), precision=highest
    )
    return ensemble + change / math.sqrt(members - 1.0)


def solution(mesh):
    finer = Mesh(
        mesh.devices.reshape(16, 4, 2, mesh.shape["mem"]), ("cells_0", "cells_1", "cells_2", "mem")
    )
    placed = (P("mem", CELLS), P(CELLS), P(CELLS), P(CELLS), P("mem"))
    return jax.shard_map(
        shards, mesh=finer, in_specs=placed, out_specs=P("mem", CELLS), check_vma=False
    )
```

profile of v0, /device:TPU:1, one launch (start us, length us, event | category | flops | bytes accessed | tf_op | source)
XLA Modules:
  0.0 412.3 jit_solution(3694493013845789510)
XLA Ops:
  8.1 5.5 %gather_fusion = f32[2048,128]{1,0:T(8,128)S(1)} fusion(f32[128,2048]{0,1:T(8,128)S(1)} %copy.68, s32[2048]{0:T(1024)S(1)} %fusion.75), kind=kCustom, calls=%fused_computation | custom fusion | bytes 2105344 | tf_op jit(solution)/shard_map/gather | solution.py:95
  15.0 9.1 %all_to_all.34 = f32[4,1,4096]{2,1,0:T(1,128)S(1)} all-to-all(f32[4,1,4096]{2,1,0:T(1,128)S(1)} %broadcast_in_dim.10), channel_id=1, replica_groups=mesh['cells_0'=16,'cells_1'=4,'cells_2'=2,'mem'=4] {'mem'}, dimensions={0} | all-to-all | bytes 131072 | tf_op jit(solution)/shard_map/all_to_all | solution.py:15
  25.8 61.8 %all-gather.3.cloned.1.call-done = f32[512,2048]{0,1:T(8,128)} async-done(((f32[128,2048]{0,1:T(8,128)}), f32[512,2048]{0,1:T(8,128)}) %all-gather.3.cloned.1.call-update) | async-done | bytes 4194320 | tf_op jit(solution)/shard_map/all_gather | solution.py:104
  87.6 10.6 %convolution_bitcast_fusion.1 = f32[64,4,8,128]{3,2,1,0:T(8,128)S(1)} fusion(f32[512,2048]{0,1:T(8,128)} %all-gather.3.cloned.1.call-done), kind=kOutput, calls=%fused_computation.7 | convolution fusion | flops 6442450944 | bytes 5242880 | tf_op jit(solution)/shard_map/dot_general | solution.py:107
  98.4 10.8 %convolution_bitcast_fusion = f32[65536]{0:T(1024)S(1)} fusion(f32[512,2048]{0,1:T(8,128)S(1)} %copy-done, f32[2048,128]{1,0:T(8,128)S(1)} %gather_fusion, f32[2048]{0:T(1024)S(1)} %copy-done.6, s32[128]{0:T(128)S(1)} %get-tuple-element.58, s32[2048]{0:T(1024)S(1)} %add_select_fusion.1, s32[128]{0:T(128)S(1)} %get-tuple-element.57, ...), kind=kOutput, calls=%fused_computation.3 | convolution fusion | flops 1614807040 | bytes 5530624 | tf_op jit(solution)/shard_map/dot_general | solution.py:108
  112.6 6.9 %all_to_all.35 = f32[2,64,2560]{2,1,0:T(8,128)S(1)} all-to-all(f32[2,64,2560]{2,1,0:T(8,128)S(1)} %copy.70), channel_id=1, replica_groups=mesh['cells_0'=16,'cells_1'=4,'cells_2'=2,'mem'=4] {'cells_2'}, dimensions={0} | all-to-all | bytes 2621440 | tf_op jit(solution)/shard_map/all_to_all | solution.py:56
  120.1 51.1 %all_to_all.36 = f32[64,1,2560]{2,1,0:T(1,128)S(1)} all-to-all(f32[64,1,2560]{2,1,0:T(1,128)S(1)} %all_to_all.24), channel_id=1, replica_groups=mesh['cells_0'=16,'cells_1'=4,'cells_2'=2,'mem'=4] {'cells_0','cells_1'}, dimensions={0} | all-to-all | bytes 1310720 | tf_op jit(solution)/shard_map/all_to_all | solution.py:64
  172.8 7.9 %all-to-all-start.3 = ((f32[64,1,2560]{2,1,0:T(1,128)}), f32[64,1,2560]{2,1,0:T(1,128)S(1)}, u32[]{:S(2)}, u32[]{:S(2)}) async-start(f32[64,1,2560]{2,1,0:T(1,128)} %broadcast_in_dim.12), calls=%async_computation.3 | async-start | bytes 1310720 | tf_op jit(solution)/shard_map/all_to_all | solution.py:15
  181.9 33.7 %all-to-all-done.3 = f32[64,1,2560]{2,1,0:T(1,128)S(1)} async-done(((f32[64,1,2560]{2,1,0:T(1,128)}), f32[64,1,2560]{2,1,0:T(1,128)S(1)}, u32[]{:S(2)}, u32[]{:S(2)}) %all-to-all-start.3) | async-done | bytes 655392 | tf_op jit(solution)/shard_map/all_to_all | solution.py:15
  215.7 8.9 %all_to_all.37 = f32[2,64,2560]{2,1,0:T(8,128)S(1)} all-to-all(f32[2,64,2560]{2,1,0:T(8,128)S(1)} %broadcast_in_dim.24), channel_id=1, replica_groups=mesh['cells_0'=16,'cells_1'=4,'cells_2'=2,'mem'=4] {'cells_2'}, dimensions={0} | all-to-all | bytes 2621440 | tf_op jit(solution)/shard_map/all_to_all | solution.py:15
  225.7 2.1 slice.179
  227.8 2.3 slice.197
  232.8 2.6 copy.73
  237.8 11.7 %cholesky.103 = f32[128,128]{1,0:T(8,128)S(1)} custom-call(f32[128,128]{1,0:T(8,128)S(1)} %cholesky.263), custom_call_target="Cholesky" | custom-call | tf_op jit(solution)/shard_map/jit(cholesky)/cholesky | solution.py:112
  249.6 9.8 %custom-call.34 = f32[1,128,128]{1,2,0:T(8,128)S(1)} custom-call(f32[1,128,128]{2,1,0:T(8,128)S(1)} %get-tuple-element.52), custom_call_target="InvertDiagBlocksLowerTriangular" | custom-call | tf_op jit(solution)/shard_map/jit(cholesky)/cholesky | solution.py:112
  262.6 11.8 %cholesky.215 = f32[128,128]{1,0:T(8,128)S(1)} custom-call(f32[128,128]{1,0:T(8,128)S(1)} %cholesky.267), custom_call_target="Cholesky" | custom-call | tf_op jit(solution)/shard_map/jit(cholesky)/cholesky | solution.py:112
  276.2 10.6 %custom-call.35 = f32[1,128,128]{1,2,0:T(8,128)S(1)} custom-call(f32[1,128,128]{2,1,0:T(8,128)} %get-tuple-element.50), custom_call_target="InvertDiagBlocksLowerTriangular" | custom-call | tf_op jit(solution)/shard_map/jit(cholesky)/cholesky | solution.py:112
  291.2 13.2 %cholesky.236 = f32[128,128]{1,0:T(8,128)} custom-call(f32[128,128]{1,0:T(8,128)} %cholesky.272), custom_call_target="Cholesky" | custom-call | tf_op jit(solution)/shard_map/jit(cholesky)/cholesky | solution.py:112
  308.2 11.3 %custom-call.36 = f32[1,128,128]{1,2,0:T(8,128)} custom-call(f32[1,128,128]{2,1,0:T(8,128)} %get-tuple-element.48), custom_call_target="InvertDiagBlocksLowerTriangular" | custom-call | tf_op jit(solution)/shard_map/jit(cholesky)/cholesky | solution.py:112
  320.6 2.1 slice.181
  324.3 11.7 %cholesky.253 = f32[128,128]{1,0:T(8,128)S(1)} custom-call(f32[128,128]{1,0:T(8,128)S(1)} %convolution_subtract_fusion.8), custom_call_target="Cholesky" | custom-call | tf_op jit(solution)/shard_map/jit(cholesky)/cholesky | solution.py:112
  341.1 10.8 %while.1 = (s32[]{:T(128)}, f32[512,512]{0,1:T(8,128)S(1)}, s32[4,2]{0,1:T(2,128)S(1)}, f32[4,128,128]{2,1,0:T(8,128)}, s32[]{:T(128)}) while((s32[]{:T(128)}, f32[512,512]{0,1:T(8,128)S(1)}, s32[4,2]{0,1:T(2,128)S(1)}, f32[4,128,128]{2,1,0:T(8,128)}, s32[]{:T(128)}) %tuple.33), condition=%wide.while_cond, body=%wide.while_body.sunk | while | flops 2 | bytes 393829 | solution.py:113
  351.9 40.4 %custom-call.37 = f32[4,128,128]{1,2,0:T(8,128)S(1)} custom-call(f32[4,128,128]{2,1,0:T(8,128)} %get-tuple-element.12), custom_call_target="InvertDiagBlocksLowerTriangular" | custom-call | tf_op jit(solution)/shard_map/jit(_cho_solve)/triangular_solve | solution.py:113
  399.7 5.5 %fusion = f32[128,2048]{1,0:T(8,128)} fusion(f32[128,2048]{1,0:T(8,128)S(1)} %copy-done.1, f32[512,2048]{1,0:T(8,128)} %all-gather.5.cloned.1.call-done, f32[128,128]{1,0:T(8,128)S(1)} %fusion.73, f32[128,128]{1,0:T(8,128)S(1)} %fusion.71, f32[128,128]{1,0:T(8,128)S(1)} %fusion.69, f32[128,128]{1,0:T(8,128)S(1)} %fusion.68), kind=kOutput, calls=%fused_computation.5 | convolution fusion | flops 1611333632 | bytes 6553600 | tf_op jit(solution)/shard_map/dot_general | solution.py:115
  (112 shorter events, 54.4 us)
Async XLA Ops:
  6.5 1.6 copy-start.4
  6.5 81.0 %all-gather.3.cloned.1.call-start = ((), (), s32[]{:S(2)}) async-start(), calls=%async_computation.5 | async-start | bytes 5242880 | tf_op jit(solution)/shard_map/all_gather | solution.py:104
  13.6 1.2 copy-start.1
  13.6 10.5 %copy-start.5 = (f32[2048]{0:T(1024)S(1)}, f32[2048]{0:T(1024)}, u32[]{:S(2)}) copy-start(f32[2048]{0:T(1024)} %param.6) | copy-start | bytes 24580
  13.6 10.5 %copy-start.6 = (f32[2048]{0:T(1024)S(1)}, f32[2048]{0:T(1024)}, u32[]{:S(2)}) copy-start(f32[2048]{0:T(1024)} %param.7) | copy-start | bytes 24580
  24.2 1.6 copy-start.7
  87.6 10.9 %copy-start = (f32[512,2048]{0,1:T(8,128)S(1)}, f32[512,2048]{0,1:T(8,128)}, u32[]{:S(2)}) copy-start(f32[512,2048]{0,1:T(8,128)} %all-gather.3.cloned.1.call-done) | copy-start | bytes 12582916
  172.8 42.8 %all-to-all-start.3 = ((f32[64,1,2560]{2,1,0:T(1,128)}), f32[64,1,2560]{2,1,0:T(1,128)S(1)}, u32[]{:S(2)}, u32[]{:S(2)}) async-start(f32[64,1,2560]{2,1,0:T(1,128)} %broadcast_in_dim.12), calls=%async_computation.3 | async-start | bytes 1310720 | tf_op jit(solution)/shard_map/all_to_all | solution.py:15
  180.7 219.0 %all-gather.5.cloned.1.call-start = ((), (), s32[]{:S(2)}) async-start(), calls=%async_computation.6 | async-start | bytes 5242880 | tf_op jit(solution)/shard_map/all_gather | solution.py:116
  236.8 1.0 copy-start.2
  261.9 0.7 copy-start.3
Sparse Core Ops, SparseCore 0:
  25.8 61.6 all-gather.2
  183.6 56.8 all-gather.4
where the time goes:
time: 418 us; the launch traced here: 412 us
  other arithmetic  132 us (32%)
  waiting for transfers between devices  95.6 us (23%)
  blocking collectives  76 us (18%)
  local copies, waits for them, and re-layouts  42.6 us (10%)
  matrix products  41.9 us (10%)
  between operations  16.5 us (4%)
  starting transfers between devices  7.93 us (2%)
    another operation x15, other arithmetic, shards(): jnp.linalg.cholesky(gram_matrix + alpha * jnp.eye(members, dtype=jnp.floa...  84.9 us
    all_gather x1, waiting for transfers between devices, shards(): gathered = lax.all_gather(scaled, 'mem', axis=0, tiled=True)  61.8 us
    all_to_all x1, blocking collectives, summed_rows(): lax.all_to_all(nearer, far, split_axis=0, concat_axis=0, tiled=True)  51.1 us
    another operation x3, other arithmetic, shards(): weights = jax.scipy.linalg.cho_solve((factor, True), cross_terms)  40.5 us
    all_to_all x1, waiting for transfers between devices, from_everyone(): return lax.all_to_all(copies, axis, split_axis=0, concat_axis=0, tiled=True)  33.7 us
    all_to_all x2, blocking collectives, from_everyone(): return lax.all_to_all(copies, axis, split_axis=0, concat_axis=0, tiled=True)  18 us
    dot_general x1, matrix products, shards(): jnp.dot(gathered, innovation.T, precision=highest)  10.8 us
    another operation x20, local copies, waits for them, and re-layouts  10.7 us
  transfers between devices with their start and end apart: 3, of which 2 were waited for; matrix products, arithmetic and copies ran while one was open for 42% of the time, Pallas kernels for 0%

commit v1 on v0

--- a/solution.py
+++ b/solution.py
@@ -101,7 +101,13 @@
     noise = perturbation(member_seeds, positions)
     scaled = (predicted - mean_pred) / (obs_sigma * math.sqrt(members - 1.0))
     innovation = observed / obs_sigma + jnp.sqrt(alpha) * noise - predicted / obs_sigma
-    gathered = lax.all_gather(scaled, "mem", axis=0, tiled=True)
+    gathered = jax.lax.all_to_all(
+        jnp.concatenate([scaled for _ in range(jax.lax.axis_size("mem"))], 0),
+        concat_axis=0,
+        tiled=True,
+        split_axis=0,
+        axis_name="mem",
+    )
     gram_matrix, cross_terms = together_2(
         (
             jnp.dot(gathered, gathered.T, precision=highest),

time: 418 us -> 413 us (0.988)
  waiting for transfers between devices: 95.6 us -> 80.7 us
  starting transfers between devices: 7.93 us -> 17.7 us
  matrix products: 41.9 us -> 37.1 us
  local copies, waits for them, and re-layouts: 42.6 us -> 47.3 us
    all_gather x1 -> x0, waiting for transfers between devices: 61.8 us -> none  [shards(): gathered = lax.all_gather(scaled, 'mem', axis=0, tiled=True)]
    all_to_all x0 -> x1, waiting for transfers between devices: none -> 42.5 us  [shards(): jax.lax.all_to_all(jnp.concatenate([scaled for _ in range(jax.lax.axis_si...]
    all_to_all x2 -> x1, blocking collectives: 18 us -> 8.93 us  [from_everyone(): return lax.all_to_all(copies, axis, split_axis=0, concat_axis=0, tiled=True)]
    all_to_all x0 -> x1, local copies, waits for them, and re-layouts: none -> 5.41 us  [shards(): jax.lax.all_to_all(jnp.concatenate([scaled for _ in range(jax.lax.axis_si...]
    all_to_all x0 -> x1, starting transfers between devices: none -> 4.99 us  [shards(): jax.lax.all_to_all(jnp.concatenate([scaled for _ in range(jax.lax.axis_si...]
    all_to_all x1, blocking collectives: 6.85 us -> 11.7 us  [summed_on_arrival(): lax.all_to_all(in_blocks(shard, dim, devices), axis, 0, 0, tiled=True)]
    all_to_all x1 -> x2, starting transfers between devices: 7.89 us -> 12.7 us  [from_everyone(): return lax.all_to_all(copies, axis, split_axis=0, concat_axis=0, tiled=True)]
    all_to_all x1 -> x2, waiting for transfers between devices: 33.7 us -> 38.2 us  [from_everyone(): return lax.all_to_all(copies, axis, split_axis=0, concat_axis=0, tiled=True)]
  transfers between devices with their start and end apart: 3 -> 4, of which waited for: 2 -> 3; matrix products, arithmetic and copies ran while one was open for 42% -> 42% of each run, Pallas kernels for 0% -> 0%
where the time goes in v1:
time: 413 us; the launch traced here: 407 us
  other arithmetic  133 us (32%)
  waiting for transfers between devices  80.7 us (20%)
  blocking collectives  74.8 us (18%)
  local copies, waits for them, and re-layouts  47.3 us (11%)
  matrix products  37.1 us (9%)
  starting transfers between devices  17.7 us (4%)
  between operations  16.8 us (4%)
    another operation x14, other arithmetic, shards(): jnp.linalg.cholesky(gram_matrix + alpha * jnp.eye(members, dtype=jnp.floa...  83.9 us
    all_to_all x1, blocking collectives, summed_rows(): lax.all_to_all(nearer, far, split_axis=0, concat_axis=0, tiled=True)  54.2 us
    all_to_all x1, waiting for transfers between devices, shards(): jax.lax.all_to_all(jnp.concatenate([scaled for _ in range(jax.lax.axis_si...  42.5 us
    another operation x3, other arithmetic, shards(): weights = jax.scipy.linalg.cho_solve((factor, True), cross_terms)  40.3 us
    all_to_all x2, waiting for transfers between devices, from_everyone(): return lax.all_to_all(copies, axis, split_axis=0, concat_axis=0, tiled=True)  38.2 us
    all_to_all x2, starting transfers between devices, from_everyone(): return lax.all_to_all(copies, axis, split_axis=0, concat_axis=0, tiled=True)  12.7 us
    all_to_all x1, blocking collectives, summed_on_arrival(): lax.all_to_all(in_blocks(shard, dim, devices), axis, 0, 0, tiled=True)  11.7 us
    another operation x20, local copies, waits for them, and re-layouts  10.9 us
  transfers between devices with their start and end apart: 4, of which 3 were waited for; matrix products, arithmetic and copies ran while one was open for 42% of the time, Pallas kernels for 0%

profile of v1, /device:TPU:1, one launch (start us, length us, event | category | flops | bytes accessed | tf_op | source)
XLA Modules:
  0.0 407.1 jit_solution(15197538853626586906)
XLA Ops:
  8.8 5.5 %gather_fusion = f32[2048,128]{1,0:T(8,128)S(1)} fusion(f32[128,2048]{0,1:T(8,128)S(1)} %copy.73, s32[2048]{0:T(1024)S(1)} %fusion.75), kind=kCustom, calls=%fused_computation | custom fusion | bytes 2105344 | tf_op jit(solution)/shard_map/gather | solution.py:95
  15.4 4.8 %all-to-all-start = ((f32[4,1,4096]{2,1,0:T(1,128)}), f32[4,1,4096]{2,1,0:T(1,128)S(1)}, u32[]{:S(2)}, u32[]{:S(2)}) async-start(f32[4,1,4096]{2,1,0:T(1,128)} %broadcast_in_dim.10), calls=%async_computation | async-start | bytes 131072 | tf_op jit(solution)/shard_map/all_to_all | solution.py:15
  20.2 4.5 %all-to-all-done = f32[4,1,4096]{2,1,0:T(1,128)S(1)} async-done(((f32[4,1,4096]{2,1,0:T(1,128)}), f32[4,1,4096]{2,1,0:T(1,128)S(1)}, u32[]{:S(2)}, u32[]{:S(2)}) %all-to-all-start) | async-done | bytes 65568 | tf_op jit(solution)/shard_map/all_to_all | solution.py:15
  27.7 5.0 %all-to-all-start.1 = ((f32[4,128,2048]{1,2,0:T(8,128)}), f32[4,128,2048]{1,2,0:T(8,128)}, u32[]{:S(2)}, u32[]{:S(2)}) async-start(f32[4,128,2048]{1,2,0:T(8,128)} %copy_bitcast_fusion), calls=%async_computation.1 | async-start | bytes 8388608 | tf_op jit(solution)/shard_map/all_to_all | solution.py:104
  32.8 42.5 %all-to-all-done.1 = f32[4,128,2048]{1,2,0:T(8,128)} async-done(((f32[4,128,2048]{1,2,0:T(8,128)}), f32[4,128,2048]{1,2,0:T(8,128)}, u32[]{:S(2)}, u32[]{:S(2)}) %all-to-all-start.1) | async-done | bytes 4194336 | tf_op jit(solution)/shard_map/all_to_all | solution.py:104
  75.3 5.4 %copy.76 = f32[4,128,2048]{2,1,0:T(8,128)} copy(f32[4,128,2048]{1,2,0:T(8,128)} %all-to-all-done.1) | data formatting | bytes 8388608 | tf_op jit(solution)/shard_map/all_to_all | solution.py:104
  80.7 9.7 %convolution_bitcast_fusion.1 = f32[64,4,8,128]{3,2,1,0:T(8,128)S(1)} fusion(f32[512,2048]{1,0:T(8,128)} %bitcast.82), kind=kOutput, calls=%fused_computation.9 | convolution fusion | flops 6442450944 | bytes 5242880 | tf_op jit(solution)/shard_map/dot_general | solution.py:113
  90.7 7.6 %convolution_bitcast_fusion = f32[65536]{0:T(1024)S(1)} fusion(f32[512,2048]{1,0:T(8,128)S(1)} %bitcast.83, f32[2048,128]{1,0:T(8,128)S(1)} %gather_fusion, f32[2048]{0:T(1024)S(1)} %copy-done.5, s32[128]{0:T(128)S(1)} %get-tuple-element.58, s32[2048]{0:T(1024)S(1)} %add_select_fusion.1, s32[128]{0:T(128)S(1)} %get-tuple-element.57, ...), kind=kOutput, calls=%fused_computation.3 | convolution fusion | flops 1614807040 | bytes 5530624 | tf_op jit(solution)/shard_map/dot_general | solution.py:114
  101.7 11.7 %all_to_all.46 = f32[2,64,2560]{2,1,0:T(8,128)S(1)} all-to-all(f32[2,64,2560]{2,1,0:T(8,128)S(1)} %copy.77), channel_id=1, replica_groups=mesh['cells_0'=16,'cells_1'=4,'cells_2'=2,'mem'=4] {'cells_2'}, dimensions={0} | all-to-all | bytes 2621440 | tf_op jit(solution)/shard_map/all_to_all | solution.py:56
  114.0 54.2 %all_to_all.47 = f32[64,1,2560]{2,1,0:T(1,128)S(1)} all-to-all(f32[64,1,2560]{2,1,0:T(1,128)S(1)} %all_to_all.35), channel_id=1, replica_groups=mesh['cells_0'=16,'cells_1'=4,'cells_2'=2,'mem'=4] {'cells_0','cells_1'}, dimensions={0} | all-to-all | bytes 1310720 | tf_op jit(solution)/shard_map/all_to_all | solution.py:64
  169.8 7.9 %all-to-all-start.4 = ((f32[64,1,2560]{2,1,0:T(1,128)}), f32[64,1,2560]{2,1,0:T(1,128)S(1)}, u32[]{:S(2)}, u32[]{:S(2)}) async-start(f32[64,1,2560]{2,1,0:T(1,128)} %broadcast_in_dim.12), calls=%async_computation.4 | async-start | bytes 1310720 | tf_op jit(solution)/shard_map/all_to_all | solution.py:15
  178.9 33.7 %all-to-all-done.4 = f32[64,1,2560]{2,1,0:T(1,128)S(1)} async-done(((f32[64,1,2560]{2,1,0:T(1,128)}), f32[64,1,2560]{2,1,0:T(1,128)S(1)}, u32[]{:S(2)}, u32[]{:S(2)}) %all-to-all-start.4) | async-done | bytes 655392 | tf_op jit(solution)/shard_map/all_to_all | solution.py:15
  212.8 8.9 %all_to_all.48 = f32[2,64,2560]{2,1,0:T(8,128)S(1)} all-to-all(f32[2,64,2560]{2,1,0:T(8,128)S(1)} %broadcast_in_dim.24), channel_id=1, replica_groups=mesh['cells_0'=16,'cells_1'=4,'cells_2'=2,'mem'=4] {'cells_2'}, dimensions={0} | all-to-all | bytes 2621440 | tf_op jit(solution)/shard_map/all_to_all | solution.py:15
  229.8 2.6 copy.80
  234.8 11.7 %cholesky.103 = f32[128,128]{1,0:T(8,128)S(1)} custom-call(f32[128,128]{1,0:T(8,128)S(1)} %cholesky.263), custom_call_target="Cholesky" | custom-call | tf_op jit(solution)/shard_map/jit(cholesky)/cholesky | solution.py:118
  246.6 9.8 %custom-call.34 = f32[1,128,128]{1,2,0:T(8,128)S(1)} custom-call(f32[1,128,128]{2,1,0:T(8,128)S(1)} %get-tuple-element.52), custom_call_target="InvertDiagBlocksLowerTriangular" | custom-call | tf_op jit(solution)/shard_map/jit(cholesky)/cholesky | solution.py:118
  258.9 11.8 %cholesky.215 = f32[128,128]{1,0:T(8,128)S(1)} custom-call(f32[128,128]{1,0:T(8,128)S(1)} %cholesky.267), custom_call_target="Cholesky" | custom-call | tf_op jit(solution)/shard_map/jit(cholesky)/cholesky | solution.py:118
  272.5 10.6 %custom-call.35 = f32[1,128,128]{1,2,0:T(8,128)S(1)} custom-call(f32[1,128,128]{2,1,0:T(8,128)} %get-tuple-element.50), custom_call_target="InvertDiagBlocksLowerTriangular" | custom-call | tf_op jit(solution)/shard_map/jit(cholesky)/cholesky | solution.py:118
  287.5 13.2 %cholesky.236 = f32[128,128]{1,0:T(8,128)} custom-call(f32[128,128]{1,0:T(8,128)} %cholesky.272), custom_call_target="Cholesky" | custom-call | tf_op jit(solution)/shard_map/jit(cholesky)/cholesky | solution.py:118
  306.7 10.6 %custom-call.36 = f32[1,128,128]{1,2,0:T(8,128)S(1)} custom-call(f32[1,128,128]{2,1,0:T(8,128)} %get-tuple-element.48), custom_call_target="InvertDiagBlocksLowerTriangular" | custom-call | tf_op jit(solution)/shard_map/jit(cholesky)/cholesky | solution.py:118
  319.2 11.7 %cholesky.253 = f32[128,128]{1,0:T(8,128)S(1)} custom-call(f32[128,128]{1,0:T(8,128)S(1)} %convolution_subtract_fusion.8), custom_call_target="Cholesky" | custom-call | tf_op jit(solution)/shard_map/jit(cholesky)/cholesky | solution.py:118
  336.0 11.0 %while.1 = (s32[]{:T(128)}, f32[512,512]{0,1:T(8,128)S(1)}, s32[4,2]{0,1:T(2,128)S(1)}, f32[4,128,128]{2,1,0:T(8,128)}, s32[]{:T(128)}) while((s32[]{:T(128)}, f32[512,512]{0,1:T(8,128)S(1)}, s32[4,2]{0,1:T(2,128)S(1)}, f32[4,128,128]{2,1,0:T(8,128)}, s32[]{:T(128)}) %tuple.32), condition=%wide.while_cond, body=%wide.while_body.sunk | while | flops 2 | bytes 393829 | solution.py:119
  347.0 40.1 %custom-call.37 = f32[4,128,128]{1,2,0:T(8,128)S(1)} custom-call(f32[4,128,128]{2,1,0:T(8,128)} %get-tuple-element.12), custom_call_target="InvertDiagBlocksLowerTriangular" | custom-call | tf_op jit(solution)/shard_map/jit(_cho_solve)/triangular_solve | solution.py:119
  394.5 5.5 %fusion = f32[128,2048]{1,0:T(8,128)} fusion(f32[128,2048]{1,0:T(8,128)S(1)} %copy-done.1, f32[512,2048]{1,0:T(8,128)} %all-gather.2.cloned.1.call-done, f32[128,128]{1,0:T(8,128)S(1)} %fusion.73, f32[128,128]{1,0:T(8,128)S(1)} %fusion.71, f32[128,128]{1,0:T(8,128)S(1)} %fusion.69, f32[128,128]{1,0:T(8,128)S(1)} %fusion.68), kind=kOutput, calls=%fused_computation.7 | convolution fusion | flops 1611333632 | bytes 6553600 | tf_op jit(solution)/shard_map/dot_general | solution.py:121
  (112 shorter events, 61.1 us)
Async XLA Ops:
  8.8 5.8 %copy-start.1 = (f32[128,2048]{1,0:T(8,128)S(1)}, f32[128,2048]{1,0:T(8,128)}, u32[]{:S(2)}) copy-start(f32[128,2048]{1,0:T(8,128)} %param.5) | copy-start | bytes 3145732
  8.8 11.4 %copy-start.4 = (f32[2048]{0:T(1024)S(1)}, f32[2048]{0:T(1024)}, u32[]{:S(2)}) copy-start(f32[2048]{0:T(1024)} %param.6) | copy-start | bytes 24580
  8.8 11.4 %copy-start.5 = (f32[2048]{0:T(1024)S(1)}, f32[2048]{0:T(1024)}, u32[]{:S(2)}) copy-start(f32[2048]{0:T(1024)} %param.7) | copy-start | bytes 24580
  15.4 9.3 %all-to-all-start = ((f32[4,1,4096]{2,1,0:T(1,128)}), f32[4,1,4096]{2,1,0:T(1,128)S(1)}, u32[]{:S(2)}, u32[]{:S(2)}) async-start(f32[4,1,4096]{2,1,0:T(1,128)} %broadcast_in_dim.10), calls=%async_computation | async-start | bytes 131072 | tf_op jit(solution)/shard_map/all_to_all | solution.py:15
  27.7 5.0 %copy-start.6 = (s32[128]{0:T(128)S(1)}, s32[128]{0:T(128)}, u32[]{:S(2)}) copy-start(s32[128]{0:T(128)} %param.9) | copy-start | bytes 1540
  27.7 47.5 %all-to-all-start.1 = ((f32[4,128,2048]{1,2,0:T(8,128)}), f32[4,128,2048]{1,2,0:T(8,128)}, u32[]{:S(2)}, u32[]{:S(2)}) async-start(f32[4,128,2048]{1,2,0:T(8,128)} %copy_bitcast_fusion), calls=%async_computation.1 | async-start | bytes 8388608 | tf_op jit(solution)/shard_map/all_to_all | solution.py:104
  80.7 10.0 %copy-start = (f32[4,128,2048]{2,1,0:T(8,128)S(1)}, f32[4,128,2048]{2,1,0:T(8,128)}, u32[]{:S(2)}) copy-start(f32[4,128,2048]{2,1,0:T(8,128)} %copy.76) | copy-start | bytes 12582916
  169.8 42.8 %all-to-all-start.4 = ((f32[64,1,2560]{2,1,0:T(1,128)}), f32[64,1,2560]{2,1,0:T(1,128)S(1)}, u32[]{:S(2)}, u32[]{:S(2)}) async-start(f32[64,1,2560]{2,1,0:T(1,128)} %broadcast_in_dim.12), calls=%async_computation.4 | async-start | bytes 1310720 | tf_op jit(solution)/shard_map/all_to_all | solution.py:15
  177.7 216.8 %all-gather.2.cloned.1.call-start = ((), (), s32[]{:S(2)}) async-start(), calls=%async_computation.6 | async-start | bytes 5242880 | tf_op jit(solution)/shard_map/all_gather | solution.py:122
  233.8 1.0 copy-start.2
  258.9 13.4 %copy-start.3 = (f32[384,128]{1,0:T(8,128)}, f32[384,128]{1,0:T(8,128)S(1)}, u32[]{:S(2)}) copy-start(f32[384,128]{1,0:T(8,128)S(1)} %convolution_subtract_fusion) | copy-start | bytes 589828
Sparse Core Ops, SparseCore 0:
  180.6 55.3 all-gather.1
